TPU v7x, 32 devices: a whole 2x2x4 slice. The times are simulated.
32 devices in a mesh: lat: 16 (over z, y, x), field: 2 (over core).
Axes of the slice: x: 2, y: 2, z: 4, core: 2. Of those that a mesh axis runs over, the one named last changes fastest.
Arguments:
- fields_grid: bfloat16 [2, 64, 2, 48, 192], P('field', None, None, 'lat'), may hold values from -6 to 6
- basis: bfloat16 [128, 48, 96], P('lat'), may hold values from -0.875 to 0.875
- order_table: int32 [16, 8], replicated, may hold values from -1 to 95, as said below
- panel_modes: int32 [2, 64], replicated, may hold values from 0 to 95, as said below
Outputs:
- panel: bfloat16 [2, 128, 192, 128], P('field', 'lat')
Inputs may be any that keep to these rules, and one draw needn't show every extreme that they name: `order_table`: each order 0 to 95 stands in exactly one slot; every other slot holds -1; some group has all 8 slots filled. `panel_modes`: row 1 is never smaller than row 0 in the same column; degree 95 appears.
All inputs are finite; a program needn't handle non-finite values.
Results may differ from a plain program's by a relative error of at most 0.0082.
Values may be sent and summed in bfloat16 or wider, within the bound.
A program may use at most 64 MiB of HBM per device.

v0:
```python
import math
import jax
import jax.numpy as jnp
from jax import lax
from jax.sharding import PartitionSpec as P


def dft_table(orders, lon_count):
    valid_slot = orders >= 0
    safe_orders = jnp.maximum(orders, 0)
    products = lax.broadcasted_iota(jnp.int32, (lon_count, 1), 0) * safe_orders[None, :] % lon_count
    angles = products.astype(jnp.float32) * (2.0 * math.pi / lon_count)
    cosine = jnp.where(valid_slot[None, :], jnp.cos(angles), 0.0).astype(jnp.bfloat16)
    sine_table = jnp.where(valid_slot[None, :], -jnp.sin(angles), 0.0).astype(jnp.bfloat16)
    return jnp.stack([cosine, sine_table], axis=1)


def local(fields_grid, basis, order_table, panel_modes):
    grid_one = fields_grid[0]
    snap_count = grid_one.shape[0]
    pair_count = grid_one.shape[2]
    lon_count = grid_one.shape[3]
    slot_count = order_table.shape[1]
    deg_count = basis.shape[2]
    pair_total = basis.shape[1]
    mode_count = panel_modes.shape[1]
    orders = order_table.reshape(-1)
    slot_all = orders.shape[0]
    dft = dft_table(orders, lon_count)
    fourier = jnp.einsum("thjn,nrk->hkjrt", grid_one, dft, preferred_element_type=jnp.float32) * (
        1.0 / math.sqrt(lon_count)
    )
    fourier = fourier.reshape(2, slot_all, pair_count, 2 * snap_count)
    parity_parts = jnp.stack([fourier[0] + fourier[1], fourier[0] - fourier[1]]).astype(
        jnp.bfloat16
    )
    group_index = lax.axis_index("lat")
    my_orders = lax.dynamic_slice_in_dim(order_table, group_index, 1, 0)[0]
    my_odd = my_orders % 2 == 1
    basis_split = basis.reshape(slot_count, pair_total, deg_count // 2, 2)
    even_rows = basis_split[:, :, :, 0]
    odd_rows = basis_split[:, :, :, 1]
    degree = lax.broadcasted_iota(jnp.int32, (1, deg_count), 1)
    keep_mask = (degree >= my_orders[:, None]) & (my_orders >= 0)[:, None]
    received = lax.all_to_all(parity_parts, "lat", split_axis=1, concat_axis=2, tiled=True)
    first_parity = jnp.where(my_odd[:, None, None], received[1], received[0])
    second = jnp.where(my_odd[:, None, None], received[0], received[1])
    low_degrees = jnp.einsum(
        "sjh,sjc->shc", even_rows, first_parity, preferred_element_type=jnp.float32
    )
    high_degrees = jnp.einsum("sjh,sjc->shc", odd_rows, second, preferred_element_type=jnp.float32)
    joined = jnp.stack([low_degrees, high_degrees], axis=2).reshape(slot_count, deg_count, -1)
    coefficients = jnp.where(keep_mask[:, :, None], joined, 0.0).astype(jnp.bfloat16)
    mode_order = panel_modes[0]
    mode_degree = panel_modes[1]
    onehot = (my_orders[None, :] == mode_order[:, None]).astype(jnp.bfloat16)
    picked = jnp.take(coefficients, mode_degree, axis=1)
    local_values = jnp.einsum("ms,smc->mc", onehot, picked, preferred_element_type=jnp.float32)
    field_index = lax.axis_index("field")
    both_fields = jnp.stack(
        [
            jnp.where(field_index == 0, local_values, 0.0),
            jnp.where(field_index == 1, local_values, 0.0),
        ]
    )
    summed = lax.psum(both_fields, ("lat", "field"))
    other_field = jnp.where(field_index == 0, summed[1], summed[0]).astype(jnp.bfloat16)
    columns = other_field.astype(jnp.float32).reshape(mode_count * 2, snap_count)
    centered = (columns - jnp.mean(columns, axis=1, keepdims=True)).astype(jnp.bfloat16)
    coef_rows = coefficients.reshape(slot_count * deg_count * 2, snap_count)
    panel_values = lax.dot_general(
        coef_rows, centered, (((1,), (1,)), ((), ())), preferred_element_type=jnp.float32
    )
    panel_values = panel_values * (1.0 / (snap_count - 1))
    return panel_values.astype(jnp.bfloat16).reshape(1, slot_count, 2 * deg_count, 2 * mode_count)


def solution(mesh):
    placed = (P("field", None, None, "lat", None), P("lat", None, None), P(), P())
    return jax.shard_map(
        local, mesh=mesh, in_specs=placed, out_specs=P("field", "lat", None, None), check_vma=False
    )
```

profile of v0, /device:TPU:0, one launch (start us, length us, event | category | flops | bytes accessed | tf_op | source)
XLA Modules:
  0.0 63.5 jit_solution(17050038539362757233)
XLA Ops:
  0.0 0.8 %broadcast_compare_fusion = pred[16,8]{0,1:T(8,128)(4,1)S(1)} fusion(s32[16,8]{0,1:T(8,128)} %param.6), kind=kLoop, calls=%fused_computation.57 | loop fusion | flops 128 | bytes 640 | tf_op jit(solution)/shard_map/ge | solution.py:9
  0.8 0.0 copy-done.1
  0.8 0.1 copy.39
  0.9 0.1 ge.51
  1.0 0.1 copy.40
  1.0 0.1 max.11
  1.1 0.4 select_convert_fusion.1
  1.6 1.1 %fusion.1 = f32[2,128,3,2,64]{1,4,2,0,3:T(8,128)S(1)} fusion(bf16[64,2,3,192]{3,1,2,0:T(2,128)(2,1)} %bitcast.69, bf16[192,1,128]{2,0,1:T(8,128)(2,1)S(1)} %get-tuple-element.16, bf16[192,1,128]{2,0,1:T(8,128)(2,1)S(1)} %get-tuple-element.15), kind=kOutput, calls=%fused_computation.4 | convolution fusion | flops 38043648 | bytes 638976 | tf_op jit(solution)/shard_map/thjn,nrk->hkjrt/dot_general | solution.py:30
  2.8 0.8 %copy.44 = bf16[2,128,3,128]{3,0,2,1:T(2,128)(2,1)} copy(bf16[2,128,3,128]{1,3,2,0:T(8,128)(2,1)S(1)} %pad_maximum_fusion.1) | data formatting | bytes 393216 | tf_op jit(solution)/shard_map/stack | solution.py:34
  3.7 8.5 %all-to-all-start = ((bf16[2,128,3,128]{3,0,2,1:T(2,128)(2,1)}), bf16[2,128,3,128]{3,0,2,1:T(2,128)(2,1)S(1)}, u32[]{:S(2)}, u32[]{:S(2)}) async-start(bf16[2,128,3,128]{3,0,2,1:T(2,128)(2,1)} %copy.44), calls=%async_computation | async-start | bytes 393216 | tf_op jit(solution)/shard_map/all_to_all | solution.py:45
  12.1 0.0 copy-start.2
  12.2 0.7 %copy-done.2 = s32[2,64]{1,0:T(2,128)S(1)} copy-done((s32[2,64]{1,0:T(2,128)S(1)}, s32[2,64]{1,0:T(2,128)}, u32[]{:S(2)}) %copy-start.2) | copy-done | bytes 536
  12.8 0.2 dynamic-slice_reduce_fusion
  13.0 0.1 compare_bitcast_fusion
  13.2 0.2 copy.48
  13.4 7.4 %all-to-all-done = bf16[2,128,3,128]{3,0,2,1:T(2,128)(2,1)S(1)} async-done(((bf16[2,128,3,128]{3,0,2,1:T(2,128)(2,1)}), bf16[2,128,3,128]{3,0,2,1:T(2,128)(2,1)S(1)}, u32[]{:S(2)}, u32[]{:S(2)}) %all-to-all-start) | async-done | bytes 196640 | tf_op jit(solution)/shard_map/all_to_all | solution.py:45
  20.9 0.1 bitcast_select_fusion.2
  21.0 0.2 convolution_bitcast_fusion.1
  21.2 0.2 convolution_bitcast_fusion
  21.4 0.1 copy.53
  21.5 0.2 fusion.2
  21.7 0.6 gather_fusion
  22.3 0.3 fusion.5
  22.6 39.0 %psum.7 = bf16[2,64,128]{2,1,0:T(8,128)(2,1)S(1)} all-reduce(f32[2,64,128]{2,1,0:T(8,128)S(1)} %pad_maximum_fusion.2), channel_id=1, replica_groups=mesh['lat'=16,'field'=2] {'lat','field'}, use_global_device_ids=true, to_apply=%region_0.1 | all-reduce | flops 16384 | bytes 98304 | tf_op jit(solution)/shard_map/psum | solution.py:66
  61.6 0.1 reshape.345
  61.7 0.1 reduce_sum.9
  61.8 0.1 div.10
  62.0 0.1 sub.26
  62.1 0.1 sub.27
  62.2 0.1 convert_element_type.92
  62.3 0.2 convert_element_type.86
  62.5 1.0 %fusion = bf16[1536,128]{1,0:T(8,128)(2,1)} fusion(bf16[1536,64]{1,0:T(8,128)(2,1)S(1)} %convert_element_type.86, bf16[128,64]{1,0:T(8,128)(2,1)S(1)} %convert_element_type.92), kind=kOutput, calls=%fused_computation.2 | convolution fusion | flops 25559040 | bytes 606208 | tf_op jit(solution)/shard_map/dot_general | solution.py:71
  (26 shorter events, 0.3 us)
Async XLA Ops:
  0.0 0.8 %copy-start.1 = (s32[16,8]{0,1:T(8,128)S(1)}, s32[16,8]{0,1:T(8,128)}, u32[]{:S(2)}) copy-start(s32[16,8]{0,1:T(8,128)} %param.6) | copy-start | bytes 1540
  3.7 9.5 %copy-start = (bf16[8,48,96]{2,1,0:T(8,128)(2,1)S(1)}, bf16[8,48,96]{2,1,0:T(8,128)(2,1)}, u32[]{:S(2)}) copy-start(bf16[8,48,96]{2,1,0:T(8,128)(2,1)} %param.5) | copy-start | bytes 221188
  3.7 17.1 %all-to-all-start = ((bf16[2,128,3,128]{3,0,2,1:T(2,128)(2,1)}), bf16[2,128,3,128]{3,0,2,1:T(2,128)(2,1)S(1)}, u32[]{:S(2)}, u32[]{:S(2)}) async-start(bf16[2,128,3,128]{3,0,2,1:T(2,128)(2,1)} %copy.44), calls=%async_computation | async-start | bytes 393216 | tf_op jit(solution)/shard_map/all_to_all | solution.py:45
  12.1 0.7 %copy-start.2 = (s32[2,64]{1,0:T(2,128)S(1)}, s32[2,64]{1,0:T(2,128)}, u32[]{:S(2)}) copy-start(s32[2,64]{1,0:T(2,128)} %param.7) | copy-start | bytes 1540
where the time goes:
time: 63.9 us; the launch traced here: 63.5 us
  blocking collectives  39 us (61%)
  starting transfers between devices  8.47 us (13%)
  waiting for transfers between devices  7.41 us (12%)
  local copies, waits for them, and re-layouts  3.74 us (6%)
  matrix products  2.79 us (4%)
  other arithmetic  1.84 us (3%)
    psum x1, blocking collectives, local(): summed = lax.psum(both_fields, ('lat', 'field'))  39 us
    all_to_all x1, starting transfers between devices, local(): lax.all_to_all(parity_parts, 'lat', split_axis=1, concat_axis=2, tiled=True)  8.47 us
    all_to_all x1, waiting for transfers between devices, local(): lax.all_to_all(parity_parts, 'lat', split_axis=1, concat_axis=2, tiled=True)  7.41 us
  transfers between devices with their start and end apart: 1, of which 1 were waited for; matrix products, arithmetic and copies ran while one was open for 1% of the time, Pallas kernels for 0%

commit v1 on v0

--- a/solution.py
+++ b/solution.py
@@ -42,7 +42,10 @@
     odd_rows = basis_split[:, :, :, 1]
     degree = lax.broadcasted_iota(jnp.int32, (1, deg_count), 1)
     keep_mask = (degree >= my_orders[:, None]) & (my_orders >= 0)[:, None]
-    received = lax.all_to_all(parity_parts, "lat", split_axis=1, concat_axis=2, tiled=True)
+    n_dev = lax.axis_size("lat")
+    blocks = jnp.stack(jnp.split(parity_parts, n_dev, axis=1), axis=0)
+    blocks = lax.all_to_all(blocks, "lat", split_axis=0, concat_axis=0)
+    received = jnp.concatenate(blocks, axis=2)
     first_parity = jnp.where(my_odd[:, None, None], received[1], received[0])
     second = jnp.where(my_odd[:, None, None], received[0], received[1])
     low_degrees = jnp.einsum(

time: 63.9 us -> 75.6 us (1.18)
  local copies, waits for them, and re-layouts: 3.74 us -> 14.4 us
  other arithmetic: 1.84 us -> 2.84 us
    unnamed x7 -> x22, local copies, waits for them, and re-layouts: 0.84 us -> 9.9 us
    another operation x3 -> x19, local copies, waits for them, and re-layouts: 0.86 us -> 2.54 us  [the longest x17 2.53 us: local(): blocks = jnp.stack(jnp.split(parity_parts, n_dev, axis=1), axis=0)]
    another operation x2 -> x3, other arithmetic: 0.06 us -> 1.07 us  [the longest x2 1.03 us: local(): blocks = jnp.stack(jnp.split(parity_parts, n_dev, axis=1), axis=0)]
    max x1, other arithmetic: 0.01 us -> 0.76 us  [dft_table(): safe_orders = jnp.maximum(orders, 0)]
    ge x1, other arithmetic: 0.76 us -> 0.01 us  [dft_table(): valid_slot = orders >= 0]
where the time goes in v1:
time: 75.6 us; the launch traced here: 75.2 us
  blocking collectives  39 us (52%)
  local copies, waits for them, and re-layouts  14.4 us (19%)
  starting transfers between devices  8.47 us (11%)
  waiting for transfers between devices  7.42 us (10%)
  other arithmetic  2.84 us (4%)
  matrix products  2.79 us (4%)
    psum x1, blocking collectives, local(): summed = lax.psum(both_fields, ('lat', 'field'))  39 us
    unnamed x22, local copies, waits for them, and re-layouts  9.9 us
    all_to_all x1, starting transfers between devices, local(): blocks = lax.all_to_all(blocks, 'lat', split_axis=0, concat_axis=0)  8.47 us
    all_to_all x1, waiting for transfers between devices, local(): blocks = lax.all_to_all(blocks, 'lat', split_axis=0, concat_axis=0)  7.42 us
    another operation x17, local copies, waits for them, and re-layouts, local(): blocks = jnp.stack(jnp.split(parity_parts, n_dev, axis=1), axis=0)  2.53 us
  transfers between devices with their start and end apart: 1, of which 1 were waited for; matrix products, arithmetic and copies ran while one was open for 1% of the time, Pallas kernels for 0%

profile of v1, /device:TPU:0, one launch (start us, length us, event | category | flops | bytes accessed | tf_op | source)
XLA Modules:
  0.0 75.2 jit_solution(9530882271355810809)
XLA Ops:
  0.0 0.8 %broadcast_maximum_fusion = s32[16,8]{0,1:T(8,128)S(1)} fusion(s32[16,8]{0,1:T(8,128)} %param.6), kind=kLoop, calls=%fused_computation.133 | loop fusion | flops 128 | bytes 1024 | tf_op jit(solution)/shard_map/max | solution.py:10
  1.1 0.4 select_convert_fusion.1
  1.6 1.1 %fusion.1 = f32[2,128,3,2,64]{1,4,2,0,3:T(8,128)S(1)} fusion(bf16[64,2,3,192]{3,1,2,0:T(2,128)(2,1)} %bitcast.101, bf16[192,1,128]{2,0,1:T(8,128)(2,1)S(1)} %get-tuple-element.32, bf16[192,1,128]{2,0,1:T(8,128)(2,1)S(1)} %get-tuple-element.31), kind=kOutput, calls=%fused_computation.4 | convolution fusion | flops 38043648 | bytes 638976 | tf_op jit(solution)/shard_map/thjn,nrk->hkjrt/dot_general | solution.py:30
  2.8 0.6 fusion.33
  3.4 0.4 fusion.4
  3.9 0.6 constant_dynamic-update-slice_fusion.15
  6.4 0.6 constant_dynamic-update-slice_fusion.14
  7.0 0.6 constant_dynamic-update-slice_fusion.13
  7.6 0.6 constant_dynamic-update-slice_fusion.12
  8.2 0.6 constant_dynamic-update-slice_fusion.11
  8.8 0.6 constant_dynamic-update-slice_fusion.10
  9.4 0.6 constant_dynamic-update-slice_fusion.9
  10.0 0.6 constant_dynamic-update-slice_fusion.8
  10.6 0.6 constant_dynamic-update-slice_fusion.7
  11.2 0.6 constant_dynamic-update-slice_fusion.6
  11.8 0.6 constant_dynamic-update-slice_fusion.5
  12.4 0.6 constant_dynamic-update-slice_fusion.4
  13.0 0.6 constant_dynamic-update-slice_fusion.3
  13.6 0.6 constant_dynamic-update-slice_fusion.2
  14.2 0.6 constant_dynamic-update-slice_fusion.1
  14.8 0.6 constant_dynamic-update-slice_fusion
  15.4 8.5 %all-to-all-start = ((bf16[16,2,8,3,128]{4,2,3,1,0:T(8,128)(2,1)}), bf16[16,2,8,3,128]{4,2,3,1,0:T(8,128)(2,1)S(1)}, u32[]{:S(2)}, u32[]{:S(2)}) async-start(bf16[16,2,8,3,128]{4,2,3,1,0:T(8,128)(2,1)} %constant_dynamic-update-slice_fusion), calls=%async_computation | async-start | bytes 393216 | tf_op jit(solution)/shard_map/all_to_all | solution.py:47
  23.9 0.7 copy-done.2
  24.6 0.2 dynamic-slice_reduce_fusion
  25.1 7.4 %all-to-all-done = bf16[16,2,8,3,128]{4,2,3,1,0:T(8,128)(2,1)S(1)} async-done(((bf16[16,2,8,3,128]{4,2,3,1,0:T(8,128)(2,1)}), bf16[16,2,8,3,128]{4,2,3,1,0:T(8,128)(2,1)S(1)}, u32[]{:S(2)}, u32[]{:S(2)}) %all-to-all-start) | async-done | bytes 196640 | tf_op jit(solution)/shard_map/all_to_all | solution.py:47
  32.7 0.2 convolution_bitcast_fusion.1
  32.9 0.2 convolution_bitcast_fusion
  33.4 0.6 gather_fusion
  34.0 0.3 fusion.36
  34.3 39.0 %psum.7 = bf16[2,64,128]{2,1,0:T(8,128)(2,1)S(1)} all-reduce(f32[2,64,128]{2,1,0:T(8,128)S(1)} %pad_maximum_fusion.2), channel_id=1, replica_groups=mesh['lat'=16,'field'=2] {'lat','field'}, use_global_device_ids=true, to_apply=%region_0.1 | all-reduce | flops 16384 | bytes 98304 | tf_op jit(solution)/shard_map/psum | solution.py:69
  74.0 0.2 convert_element_type.86
  74.2 1.0 %fusion = bf16[1536,128]{1,0:T(8,128)(2,1)} fusion(bf16[1536,64]{1,0:T(8,128)(2,1)S(1)} %convert_element_type.86, bf16[128,64]{1,0:T(8,128)(2,1)S(1)} %convert_element_type.92), kind=kOutput, calls=%fused_computation.2 | convolution fusion | flops 25559040 | bytes 606208 | tf_op jit(solution)/shard_map/dot_general | solution.py:74
  (56 shorter events, 3.7 us)
Async XLA Ops:
  0.0 0.8 %copy-start.1 = (s32[16,8]{0,1:T(8,128)S(1)}, s32[16,8]{0,1:T(8,128)}, u32[]{:S(2)}) copy-start(s32[16,8]{0,1:T(8,128)} %param.6) | copy-start | bytes 1540
  15.4 9.5 %copy-start = (bf16[8,48,96]{2,1,0:T(8,128)(2,1)S(1)}, bf16[8,48,96]{2,1,0:T(8,128)(2,1)}, u32[]{:S(2)}) copy-start(bf16[8,48,96]{2,1,0:T(8,128)(2,1)} %param.5) | copy-start | bytes 221188
  15.4 17.1 %all-to-all-start = ((bf16[16,2,8,3,128]{4,2,3,1,0:T(8,128)(2,1)}), bf16[16,2,8,3,128]{4,2,3,1,0:T(8,128)(2,1)S(1)}, u32[]{:S(2)}, u32[]{:S(2)}) async-start(bf16[16,2,8,3,128]{4,2,3,1,0:T(8,128)(2,1)} %constant_dynamic-update-slice_fusion), calls=%async_computation | async-start | bytes 393216 | tf_op jit(solution)/shard_map/all_to_all | solution.py:47
  23.9 0.7 copy-start.2
